TPU v7x, 256 devices: a whole 4x4x8 slice. The times are simulated.
256 devices in a mesh: dp: 8 (over x, core), cut: 32 (over y, z).
Axes of the slice: x: 4, y: 4, z: 8, core: 2. Of those that a mesh axis runs over, the one named last changes fastest.
Arguments:
- node_feat: bfloat16 [128, 262144], P(None, ('dp', 'cut')), parts along dimension 1, may hold values from -6 to 6
- edge_feat: bfloat16 [128, 1048576], P(None, ('dp', 'cut')), parts along dimension 1, may hold values from -6 to 6
- route: int32 [256, 32, 128], P(('dp', 'cut')), parts along dimension 0, may hold values from 0 to 1023, as said below
- block_tile: int32 [8192, 2], P(('dp', 'cut')), parts along dimension 0, may hold values from 0 to 39
- block_offset: int32 [8192, 2, 128], P(('dp', 'cut')), parts along dimension 0, may hold values from 0 to 127
- block_count: int32 [8192], P(('dp', 'cut')), parts along dimension 0, may hold values from 1 to 128, as said below
- w_edge1: bfloat16 [128, 384], replicated, may hold values from -0.3125 to 0.3125
- bias_edge1: float32 [128], replicated, may hold values from -3 to 3
- w_edge2: bfloat16 [128, 128], replicated, may hold values from -0.5 to 0.5
- gain_edge: float32 [128], replicated, may hold values from 0.1 to 1.9
- shift_edge: float32 [128], replicated, may hold values from -3 to 3
- w_node1: bfloat16 [128, 256], replicated, may hold values from -0.375 to 0.375
- bias_node1: float32 [128], replicated, may hold values from -3 to 3
- w_node2: bfloat16 [128, 128], replicated, may hold values from -0.5 to 0.5
- gain_node: float32 [128], replicated, may hold values from 0.1 to 1.9
- shift_node: float32 [128], replicated, may hold values from -3 to 3
- node_cot: bfloat16 [128, 262144], P(None, ('dp', 'cut')), parts along dimension 1, may hold values from -6 to 6
Outputs:
- node_out: bfloat16 [128, 262144], P(None, ('dp', 'cut')), parts along dimension 1
- node_grad: float32 [128, 262144], P(None, ('dp', 'cut')), parts along dimension 1
- edge_grad: bfloat16 [128, 1048576], P(None, ('dp', 'cut')), parts along dimension 1
- param_grad: float32 [923648], P('dp'), parts along dimension 0
There are 8 independent parts, one for each index of `dp`. A program takes and returns all parts, laid end to end along the dimension named above; an argument that names none is the same for every part. Nothing has to cross between parts.
Inputs may be any that keep to these rules, and one draw needn't show every extreme that they name: route[c, p, :] holds 128 distinct master rows of partition p. `block_count`: the first block of each partition is full.
All inputs are finite; a program needn't handle non-finite values.
Results may differ from a plain program's by a relative error of at most 0.024.
Values may be sent and summed in bfloat16 or wider, within the bound.
No kernel may reach another device: no remote copies, remote signals or barrier semaphores. Data moves between devices by JAX's collectives and lax.ppermute only.
A program may use at most 128 MiB of HBM per device.

v0:
```python
import math
import jax
import jax.numpy as jnp
from jax import lax
from jax.sharding import PartitionSpec as P


def silu_slope(values):
    sigmoid_val = jax.nn.sigmoid(values)
    return sigmoid_val * (1.0 + values * (1.0 - sigmoid_val))


def layer_norm(values):
    centred = values - jnp.mean(values, axis=0, keepdims=True)
    inverse = lax.rsqrt(jnp.mean(centred * centred, axis=0, keepdims=True) + 1e-05)
    return (centred * inverse, inverse)


def norm_back(upstream, normed, inverse, gain_vec):
    scaled = upstream * gain_vec[:, None]
    return inverse * (
        scaled
        - jnp.mean(scaled, axis=0, keepdims=True)
        - normed * jnp.mean(scaled * normed, axis=0, keepdims=True)
    )


def row_contract(left, right):
    return lax.dot_general(
        left, right, (((1,), (1,)), ((), ())), preferred_element_type=jnp.float32
    )


def lead_contract(weight, values):
    return lax.dot_general(
        weight, values, (((0,), (0,)), ((), ())), preferred_element_type=jnp.float32
    )


def per_device(
    node_feat,
    edge_feat,
    route,
    block_tile,
    block_offset,
    block_count,
    w_edge1,
    bias_edge1,
    w_edge2,
    gain_edge,
    shift_edge,
    w_node1,
    bias_node1,
    w_node2,
    gain_node,
    shift_node,
    node_cot,
):
    latent = node_feat.shape[0]
    masters = node_feat.shape[1]
    peer_count = lax.axis_size("cut")
    total_nodes = masters * peer_count
    total_edges = edge_feat.shape[1] * peer_count
    mirror_index = lax.all_to_all(route[0], "cut", split_axis=0, concat_axis=0, tiled=True).reshape(
        -1
    )

    def fetch_mirrors(master_part):
        outgoing = jnp.take(master_part, mirror_index, axis=1)
        result = lax.all_to_all(outgoing, "cut", split_axis=1, concat_axis=1, tiled=True)
        return result

    def reduce_mirrors(master_part, mirror_part):
        returned = lax.all_to_all(
            mirror_part.astype(jnp.bfloat16), "cut", split_axis=1, concat_axis=1, tiled=True
        ).astype(mirror_part.dtype)
        result = master_part.at[:, mirror_index].add(returned)
        return result

    columns = 128 * block_tile[:, :, None] + block_offset
    send_cols = columns[:, 0, :].reshape(-1)
    recv_cols = columns[:, 1, :].reshape(-1)
    live_mask = (
        (jnp.arange(block_offset.shape[2], dtype=jnp.int32)[None, :] < block_count[:, None])
        .reshape(-1)
        .astype(jnp.float32)
    )
    node_table = jnp.concatenate([node_feat, fetch_mirrors(node_feat)], axis=1)
    local_width = node_table.shape[1]
    stacked = jnp.concatenate(
        [
            edge_feat,
            jnp.take(node_table, send_cols, axis=1),
            jnp.take(node_table, recv_cols, axis=1),
        ],
        axis=0,
    )
    edge_pre = jnp.dot(w_edge1, stacked, preferred_element_type=jnp.float32) + bias_edge1[:, None]
    edge_hidden = jax.nn.silu(edge_pre).astype(jnp.bfloat16)
    edge_post = jnp.dot(w_edge2, edge_hidden, preferred_element_type=jnp.float32)
    edge_normed, edge_inv = layer_norm(edge_post)
    message = (gain_edge[:, None] * edge_normed + shift_edge[:, None]) * live_mask[None, :]
    local_sums = jnp.zeros((latent, local_width), jnp.float32).at[:, recv_cols].add(message)
    aggregate = reduce_mirrors(local_sums[:, :masters], local_sums[:, masters:])
    agg_low = aggregate.astype(jnp.bfloat16)
    node_input = jnp.concatenate([node_feat, agg_low], axis=0)
    node_pre = (
        jnp.dot(w_node1, node_input, preferred_element_type=jnp.float32) + bias_node1[:, None]
    )
    node_hidden = jax.nn.silu(node_pre).astype(jnp.bfloat16)
    node_post = jnp.dot(w_node2, node_hidden, preferred_element_type=jnp.float32)
    node_normed, node_inv = layer_norm(node_post)
    node_out = (
        node_feat.astype(jnp.float32) + gain_node[:, None] * node_normed + shift_node[:, None]
    ).astype(jnp.bfloat16)
    upstream = node_cot.astype(jnp.float32)
    grad_gain_node = jnp.sum(upstream * node_normed, axis=1)
    grad_shift_node = jnp.sum(upstream, axis=1)
    grad_node_post = norm_back(upstream, node_normed, node_inv, gain_node).astype(jnp.bfloat16)
    grad_w_node2 = row_contract(grad_node_post, node_hidden)
    grad_node_full = lead_contract(w_node2, grad_node_post) * silu_slope(node_pre)
    grad_node_pre = grad_node_full.astype(jnp.bfloat16)
    grad_w_node1 = row_contract(grad_node_pre, node_input)
    grad_bias_node1 = jnp.sum(grad_node_full, axis=1)
    node_direct = lead_contract(w_node1[:, :latent], grad_node_pre)
    grad_agg = lead_contract(w_node1[:, latent:], grad_node_pre).astype(jnp.bfloat16)
    node_vec = jnp.concatenate(
        [
            grad_w_node1.reshape(-1),
            grad_bias_node1,
            grad_w_node2.reshape(-1),
            grad_gain_node,
            grad_shift_node,
        ]
    )
    agg_table = jnp.concatenate([grad_agg, fetch_mirrors(grad_agg)], axis=1)
    grad_message = jnp.take(agg_table, recv_cols, axis=1).astype(jnp.float32) * live_mask[None, :]
    grad_gain_edge = jnp.sum(grad_message * edge_normed, axis=1)
    grad_shift_edge = jnp.sum(grad_message, axis=1)
    grad_edge_post = norm_back(grad_message, edge_normed, edge_inv, gain_edge).astype(jnp.bfloat16)
    grad_w_edge2 = row_contract(grad_edge_post, edge_hidden)
    grad_edge_full = lead_contract(w_edge2, grad_edge_post) * silu_slope(edge_pre)
    grad_edge_pre = grad_edge_full.astype(jnp.bfloat16)
    grad_w_edge1 = row_contract(grad_edge_pre, stacked)
    grad_bias_edge1 = jnp.sum(grad_edge_full, axis=1)
    edge_grad = lead_contract(w_edge1[:, :latent], grad_edge_pre).astype(jnp.bfloat16)
    grad_send = lead_contract(w_edge1[:, latent : 2 * latent], grad_edge_pre)
    grad_recv = lead_contract(w_edge1[:, 2 * latent :], grad_edge_pre)
    grad_table = (
        jnp.zeros((latent, local_width), jnp.float32)
        .at[:, send_cols]
        .add(grad_send)
        .at[:, recv_cols]
        .add(grad_recv)
    )
    node_grad = (
        upstream + node_direct + reduce_mirrors(grad_table[:, :masters], grad_table[:, masters:])
    )
    edge_vec = jnp.concatenate(
        [
            grad_w_edge1.reshape(-1),
            grad_bias_edge1,
            grad_w_edge2.reshape(-1),
            grad_gain_edge,
            grad_shift_edge,
        ]
    )
    summed = lax.psum(jnp.concatenate([edge_vec, node_vec]).astype(jnp.bfloat16), "cut").astype(
        jnp.float32
    )
    edge_summed = summed[: edge_vec.shape[0]]
    node_summed = summed[edge_vec.shape[0] :]
    param_grad = jnp.concatenate(
        [edge_summed / math.sqrt(total_edges), node_summed / math.sqrt(total_nodes)]
    )
    return (node_out, node_grad, edge_grad, param_grad)


def solution(mesh):
    in_specs = (
        P(None, ("dp", "cut")),
        P(None, ("dp", "cut")),
        P(("dp", "cut"), None, None),
        P(("dp", "cut"), None),
        P(("dp", "cut"), None, None),
        P(("dp", "cut")),
        P(),
        P(),
        P(),
        P(),
        P(),
        P(),
        P(),
        P(),
        P(),
        P(),
        P(None, ("dp", "cut")),
    )
    out_specs = (P(None, ("dp", "cut")), P(None, ("dp", "cut")), P(None, ("dp", "cut")), P("dp"))
    return jax.shard_map(
        per_device, mesh=mesh, in_specs=in_specs, out_specs=out_specs, check_vma=False
    )
```

profile of v0, /device:TPU:2, one launch (start us, length us, event | category | flops | bytes accessed | tf_op | source)
XLA Modules:
  0.0 506.6 jit_solution(10482661762203878273)
XLA Ops:
  7.2 11.5 %all-to-all-start = ((s32[32,1,128]{2,1,0:T(1,128)}), s32[32,1,128]{2,1,0:T(1,128)S(1)}, u32[]{:S(2)}, u32[]{:S(2)}) async-start(s32[32,1,128]{2,1,0:T(1,128)} %bitcast.144), calls=%async_computation | async-start | bytes 32768 | tf_op jit(solution)/shard_map/all_to_all | solution.py:64
  19.5 0.9 broadcast_add_fusion
  20.3 1.1 copy.38
  21.4 7.0 %all-to-all-done = s32[32,1,128]{2,1,0:T(1,128)S(1)} async-done(((s32[32,1,128]{2,1,0:T(1,128)}), s32[32,1,128]{2,1,0:T(1,128)S(1)}, u32[]{:S(2)}, u32[]{:S(2)}) %all-to-all-start) | async-done | bytes 16416 | tf_op jit(solution)/shard_map/all_to_all | solution.py:64
  28.4 12.1 %gather_fusion = bf16[4096,128]{1,0:T(8,128)(2,1)S(1)} fusion(bf16[128,1024]{0,1:T(8,128)(2,1)S(1)} %copy.38, s32[4096]{0:T(1024)S(1)} %fusion.48), kind=kCustom, calls=%fused_computation.clone | custom fusion | bytes 2113536 | tf_op jit(solution)/shard_map/jit(_take)/gather | solution.py:69
  40.6 2.9 broadcast_select_fusion.1
  43.5 3.9 all-to-all-start.1
  47.5 1.3 copy.36
  49.6 25.4 %all-to-all-done.1 = bf16[128,32,128]{0,2,1:T(8,128)(2,1)S(1)} async-done(((bf16[128,32,128]{0,2,1:T(8,128)(2,1)}), bf16[128,32,128]{0,2,1:T(8,128)(2,1)S(1)}, u32[]{:S(2)}, u32[]{:S(2)}) %all-to-all-start.1) | async-done | bytes 1048608 | tf_op jit(solution)/shard_map/all_to_all | solution.py:70
  75.1 12.1 %gather_fusion.1 = bf16[4096,128]{1,0:T(8,128)(2,1)S(1)} fusion(bf16[128,5120]{0,1:T(8,128)(2,1)S(1)} %pad_maximum_fusion.1, s32[4096]{0:T(1024)S(1)} %fusion.49), kind=kCustom, calls=%fused_computation.1.clone | custom fusion | bytes 2113536 | tf_op jit(solution)/shard_map/jit(_take)/gather | solution.py:93
  87.2 15.0 %gather_fusion.2 = bf16[4096,128]{1,0:T(8,128)(2,1)} fusion(bf16[128,5120]{0,1:T(8,128)(2,1)S(1)} %pad_maximum_fusion.1, s32[4096]{0:T(1024)S(1)} %fusion.50), kind=kCustom, calls=%fused_computation.3.clone | custom fusion | bytes 2113536 | tf_op jit(solution)/shard_map/jit(_take)/gather | solution.py:94
  102.3 3.1 select_bitcast_fusion
  105.4 2.3 multiply_convert_fusion
  109.9 1.8 copy.37
  111.8 23.3 %scatter_custom_fusion = f32[128,5120]{0,1:T(8,128)S(1)} fusion(s32[4096]{0:T(1024)S(1)} %bitcast.142, f32[4096,128]{1,0:T(8,128)} %copy.37, f32[]{:T(128)} %constant.26.clone.1), kind=kCustom, calls=%fused_computation.47 | custom fusion | flops 524288 | bytes 2621952 | tf_op jit(solution)/shard_map/scatter-add | solution.py:103
  135.1 1.1 slice.89
  136.2 5.1 %all-to-all-start.2 = ((bf16[128,32,128]{0,2,1:T(8,128)(2,1)}), bf16[128,32,128]{0,2,1:T(8,128)(2,1)}, u32[]{:S(2)}, u32[]{:S(2)}) async-start(bf16[128,32,128]{0,2,1:T(8,128)(2,1)} %bitcast.134), calls=%async_computation.2 | async-start | bytes 2097152 | tf_op jit(solution)/shard_map/all_to_all | solution.py:74
  141.4 27.5 %all-to-all-done.2 = bf16[128,32,128]{0,2,1:T(8,128)(2,1)} async-done(((bf16[128,32,128]{0,2,1:T(8,128)(2,1)}), bf16[128,32,128]{0,2,1:T(8,128)(2,1)}, u32[]{:S(2)}, u32[]{:S(2)}) %all-to-all-start.2) | async-done | bytes 1048608 | tf_op jit(solution)/shard_map/all_to_all | solution.py:74
  168.9 23.1 %scatter_custom_fusion.1 = f32[128,1024]{0,1:T(8,128)S(1)} fusion(f32[128,1024]{0,1:T(8,128)S(1)} %slice.66, s32[4096]{0:T(1024)S(1)} %bitcast.145, bf16[128,4096]{0,1:T(8,128)(2,1)} %bitcast.39), kind=kCustom, calls=%fused_computation.22 | custom fusion | flops 1048576 | bytes 1572864 | tf_op jit(solution)/shard_map/scatter-add | solution.py:77
  192.2 1.2 multiply_convert_fusion.1
  194.6 1.0 fusion.35
  195.6 0.9 fusion.62
  196.7 12.1 %gather_fusion.3 = bf16[4096,128]{1,0:T(8,128)(2,1)S(1)} fusion(bf16[128,1024]{0,1:T(8,128)(2,1)S(1)} %fusion.25, s32[4096]{0:T(1024)S(1)} %fusion.48), kind=kCustom, calls=%fused_computation.2.clone | custom fusion | bytes 2113536 | tf_op jit(solution)/shard_map/jit(_take)/gather | solution.py:69
  208.8 2.9 broadcast_select_fusion
  211.7 5.0 all-to-all-start.3
  217.8 0.8 fusion.29
  218.6 25.7 %all-to-all-done.3 = bf16[128,32,128]{0,2,1:T(8,128)(2,1)S(1)} async-done(((bf16[128,32,128]{0,2,1:T(8,128)(2,1)}), bf16[128,32,128]{0,2,1:T(8,128)(2,1)S(1)}, u32[]{:S(2)}, u32[]{:S(2)}) %all-to-all-start.3) | async-done | bytes 1048608 | tf_op jit(solution)/shard_map/all_to_all | solution.py:70
  244.4 15.0 %gather_fusion.4 = bf16[4096,128]{1,0:T(8,128)(2,1)} fusion(bf16[128,5120]{0,1:T(8,128)(2,1)S(1)} %pad_maximum_fusion.2, s32[4096]{0:T(1024)S(1)} %copy-done.18), kind=kCustom, calls=%fused_computation.4.clone | custom fusion | bytes 2113536 | tf_op jit(solution)/shard_map/jit(_take)/gather | solution.py:137
  259.5 1.6 copy.40
  261.4 2.5 fusion.12
  265.5 1.2 copy-done.41
  266.7 1.5 fusion.58
  268.5 1.4 fusion.26
  269.9 1.4 fusion.2
  271.3 1.8 fusion.42
  273.1 1.7 fusion.44
  274.8 23.3 %scatter_custom_fusion.2 = f32[128,5120]{0,1:T(8,128)S(1)} fusion(s32[4096]{0:T(1024)} %bitcast.147, f32[4096,128]{1,0:T(8,128)} %fusion.44, f32[]{:T(128)} %constant.26.clone.1), kind=kCustom, calls=%fused_computation.45 | custom fusion | flops 524288 | bytes 2621952 | tf_op jit(solution)/shard_map/scatter-add | solution.py:152
  298.1 23.8 %scatter_fusion = f32[128,5120]{0,1:T(8,128)S(1)} fusion(f32[128,5120]{0,1:T(8,128)S(1)} %scatter_custom_fusion.2, s32[4096]{0:T(1024)S(1)} %bitcast.143, f32[4096,128]{1,0:T(8,128)} %fusion.42), kind=kCustom, calls=%fused_computation.8 | custom fusion | flops 524288 | bytes 6307840 | tf_op jit(solution)/shard_map/scatter-add | solution.py:154
  322.0 1.1 slice.88
  323.1 1.0 reshape.207
  326.8 0.8 dynamic-update-slice.6
  327.6 1.1 dynamic-update-slice.7
  329.9 2.3 copy.44
  332.8 5.0 all-to-all-start.4
  337.8 136.4 %all-reduce.2.cloned.1.call-done = bf16[115456]{0:T(1024)(128)(2,1)} async-done(((bf16[115456]{0:T(1024)(128)(2,1)}), bf16[115456]{0:T(1024)(128)(2,1)}) %all-reduce.2.cloned.1.call-update) | async-done | bytes 230928 | tf_op jit(solution)/shard_map/psum | solution.py:168
  474.2 1.0 convert_element_type.94
  476.1 22.7 %scatter_custom_fusion.4 = f32[128,1024]{0,1:T(8,128)S(1)} fusion(f32[128,1024]{0,1:T(8,128)S(1)} %copy.42, s32[4096]{0:T(1024)} %bitcast.146, bf16[128,4096]{0,1:T(8,128)(2,1)S(1)} %bitcast.132), kind=kCustom, calls=%fused_computation.20 | custom fusion | flops 1048576 | bytes 1572864 | tf_op jit(solution)/shard_map/scatter-add | solution.py:77
  498.8 1.0 copy.43
  (137 shorter events, 14.1 us)
Async XLA Ops:
  7.2 100.6 %copy-start = (bf16[128,128]{1,0:T(8,128)(2,1)S(1)}, bf16[128,128]{1,0:T(8,128)(2,1)}, u32[]{:S(2)}) copy-start(bf16[128,128]{1,0:T(8,128)(2,1)} %param.29) | copy-start | bytes 98308
  7.2 21.2 %all-to-all-start = ((s32[32,1,128]{2,1,0:T(1,128)}), s32[32,1,128]{2,1,0:T(1,128)S(1)}, u32[]{:S(2)}, u32[]{:S(2)}) async-start(s32[32,1,128]{2,1,0:T(1,128)} %bitcast.144), calls=%async_computation | async-start | bytes 32768 | tf_op jit(solution)/shard_map/all_to_all | solution.py:64
  40.6 6.8 %copy-start.38 = (s32[32]{0:T(128)S(1)}, s32[32]{0:T(128)}, u32[]{:S(2)}) copy-start(s32[32]{0:T(128)} %param.26) | copy-start | bytes 388
  40.6 6.9 %copy-start.8 = (bf16[128,4096]{1,0:T(8,128)(2,1)S(1)}, bf16[128,4096]{1,0:T(8,128)(2,1)}, u32[]{:S(2)}) copy-start(bf16[128,4096]{1,0:T(8,128)(2,1)} %param.22) | copy-start | bytes 3145732
  43.5 31.5 %all-to-all-start.1 = ((bf16[128,32,128]{0,2,1:T(8,128)(2,1)}), bf16[128,32,128]{0,2,1:T(8,128)(2,1)S(1)}, u32[]{:S(2)}, u32[]{:S(2)}) async-start(bf16[128,32,128]{0,2,1:T(8,128)(2,1)} %bitcast.6), calls=%async_computation.1 | async-start | bytes 2097152 | tf_op jit(solution)/shard_map/all_to_all | solution.py:70
  48.9 53.4 %copy-start.25 = (pred[4096]{0:T(1024)(128)(4,1)}, pred[4096]{0:T(1024)(128)(4,1)S(1)}, u32[]{:S(2)}) copy-start(pred[4096]{0:T(1024)(128)(4,1)S(1)} %compare_and_fusion) | copy-start | bytes 12292
  48.9 38.3 %copy-start.17 = (s32[4096]{0:T(1024)}, s32[4096]{0:T(1024)S(1)}, u32[]{:S(2)}) copy-start(s32[4096]{0:T(1024)S(1)} %fusion.50) | copy-start | bytes 49156
  49.6 62.2 %copy-start.21 = (s32[4096,1]{0,1:T(1,128)}, s32[4096,1]{0,1:T(1,128)S(1)}, u32[]{:S(2)}) copy-start(s32[4096,1]{0,1:T(1,128)S(1)} %get-tuple-element.26) | copy-start | bytes 49156
  102.3 3.1 copy-start.9
  102.3 3.1 copy-start.19
  102.3 3.1 copy-start.39
  105.4 2.4 copy-start.12
  105.4 2.3 copy-start.14
  107.7 1.0 copy-start.3
  107.7 1.8 copy-start.29
  107.7 1.8 copy-start.36
  108.2 1.3 copy-start.1
  136.2 32.8 %all-to-all-start.2 = ((bf16[128,32,128]{0,2,1:T(8,128)(2,1)}), bf16[128,32,128]{0,2,1:T(8,128)(2,1)}, u32[]{:S(2)}, u32[]{:S(2)}) async-start(bf16[128,32,128]{0,2,1:T(8,128)(2,1)} %bitcast.134), calls=%async_computation.2 | async-start | bytes 2097152 | tf_op jit(solution)/shard_map/all_to_all | solution.py:74
  141.3 50.8 %copy-start.40 = (f32[128]{0:T(128)S(1)}, f32[128]{0:T(128)}, u32[]{:S(2)}) copy-start(f32[128]{0:T(128)} %param.33) | copy-start | bytes 1540
  141.4 52.1 %copy-start.28 = (s32[4096,1]{0,1:T(1,128)}, s32[4096,1]{0,1:T(1,128)S(1)}, u32[]{:S(2)}) copy-start(s32[4096,1]{0,1:T(1,128)S(1)} %compare_select_fusion.1) | copy-start | bytes 49156
  192.1 1.3 copy-start.27
  192.1 1.6 copy-start.5
  192.2 1.6 copy-start.31
  192.2 2.4 copy-start.11
  192.2 2.4 copy-start.37
  194.6 1.9 copy-start.23
  196.5 21.0 %copy-start.6 = (bf16[128,1024]{0,1:T(8,128)(2,1)}, bf16[128,1024]{0,1:T(8,128)(2,1)S(1)}, u32[]{:S(2)}) copy-start(bf16[128,1024]{0,1:T(8,128)(2,1)S(1)} %get-tuple-element.39) | copy-start | bytes 786436
  211.7 32.6 %all-to-all-start.3 = ((bf16[128,32,128]{0,2,1:T(8,128)(2,1)}), bf16[128,32,128]{0,2,1:T(8,128)(2,1)S(1)}, u32[]{:S(2)}, u32[]{:S(2)}) async-start(bf16[128,32,128]{0,2,1:T(8,128)(2,1)} %bitcast.28), calls=%async_computation.3 | async-start | bytes 2097152 | tf_op jit(solution)/shard_map/all_to_all | solution.py:70
  216.7 257.5 %all-reduce.2.cloned.1.call-start = ((), (), s32[]{:S(2)}) async-start(), calls=%async_computation.5 | async-start | bytes 462848 | tf_op jit(solution)/shard_map/psum | solution.py:168
  217.4 27.0 %copy-start.18 = (s32[4096]{0:T(1024)S(1)}, s32[4096]{0:T(1024)}, u32[]{:S(2)}) copy-start(s32[4096]{0:T(1024)} %copy-done.17) | copy-start | bytes 49156
  259.5 1.9 copy-start.2
  261.4 2.5 copy-start.26
  261.4 2.5 copy-start.30
  263.8 1.2 copy-start.4
  265.1 1.6 copy-start.41
  266.7 1.5 copy-start.10
  266.7 1.5 copy-start.13
  266.7 1.9 copy-start.15
  268.5 1.4 copy-start.20
  274.8 23.3 %copy-start.22 = (s32[4096,1]{0,1:T(1,128)S(1)}, s32[4096,1]{0,1:T(1,128)}, u32[]{:S(2)}) copy-start(s32[4096,1]{0,1:T(1,128)} %copy-done.21) | copy-start | bytes 49156
  322.0 3.5 copy-start.35
  322.0 3.8 copy-start.34
  322.0 6.7 %copy-start.32 = (bf16[128]{0:T(256)(128)(2,1)S(1)}, bf16[128]{0:T(256)(128)(2,1)}, u32[]{:S(2)}) copy-start(bf16[128]{0:T(256)(128)(2,1)} %get-tuple-element.18) | copy-start | bytes 772
  322.0 7.0 %copy-start.33 = (bf16[128]{0:T(256)(128)(2,1)S(1)}, bf16[128]{0:T(256)(128)(2,1)}, u32[]{:S(2)}) copy-start(bf16[128]{0:T(256)(128)(2,1)} %reduce.4) | copy-start | bytes 772
  323.1 9.2 %copy-start.7 = (bf16[128,1024]{0,1:T(8,128)(2,1)S(1)}, bf16[128,1024]{0,1:T(8,128)(2,1)}, u32[]{:S(2)}) copy-start(bf16[128,1024]{0,1:T(8,128)(2,1)} %copy-done.6) | copy-start | bytes 786436
  323.1 9.2 %copy-start.24 = (bf16[128,256]{1,0:T(8,128)(2,1)S(1)}, bf16[128,256]{1,0:T(8,128)(2,1)}, u32[]{:S(2)}) copy-start(bf16[128,256]{1,0:T(8,128)(2,1)} %param.32) | copy-start | bytes 196612
  329.1 0.7 copy-start.16
  332.8 143.2 %all-to-all-start.4 = ((bf16[128,32,128]{0,2,1:T(8,128)(2,1)}), bf16[128,32,128]{0,2,1:T(8,128)(2,1)S(1)}, u32[]{:S(2)}, u32[]{:S(2)}) async-start(bf16[128,32,128]{0,2,1:T(8,128)(2,1)} %bitcast.32), calls=%async_computation.4 | async-start | bytes 2097152 | tf_op jit(solution)/shard_map/all_to_all | solution.py:74
Sparse Core Ops, SparseCore 0:
  330.0 144.1 all-reduce.1
where the time goes:
time: 508 us; the launch traced here: 507 us
  waiting for transfers between devices  222 us (44%)
  other arithmetic  136 us (27%)
  local copies, waits for them, and re-layouts  88.5 us (17%)
  starting transfers between devices  30.5 us (6%)
  matrix products  14.8 us (3%)
  between operations  14.8 us (3%)
    psum x1, waiting for transfers between devices, per_device(): lax.psum(jnp.concatenate([edge_vec, node_vec]).astype(jnp.bfloat16), 'cut')  136 us
    all_to_all x2, waiting for transfers between devices, fetch_mirrors(): lax.all_to_all(outgoing, 'cut', split_axis=1, concat_axis=1, tiled=True)  51.1 us
    scatter-add x2, other arithmetic, per_device(): grad_table = jnp.zeros((latent, local_width), jnp.float32).at[:, send_col...  47.1 us
    scatter-add x2, other arithmetic, reduce_mirrors(): result = master_part.at[:, mirror_index].add(returned)  45.9 us
    all_to_all x2, waiting for transfers between devices, reduce_mirrors(): lax.all_to_all(mirror_part.astype(jnp.bfloat16), 'cut', split_axis=1, con...  27.5 us
    gather x2, local copies, waits for them, and re-layouts, fetch_mirrors(): outgoing = jnp.take(master_part, mirror_index, axis=1)  24.3 us
    scatter-add x1, other arithmetic, per_device(): jnp.zeros((latent, local_width), jnp.float32).at[:, recv_cols].add(message)  23.3 us
    gather x2, local copies, waits for them, and re-layouts, per_device(): jnp.take(agg_table, recv_cols, axis=1).astype(jnp.float32)  16.7 us
  transfers between devices with their start and end apart: 6, of which 5 were waited for; matrix products, arithmetic and copies ran while one was open for 2% of the time, Pallas kernels for 0%

commit v1 on v0

--- a/solution.py
+++ b/solution.py
@@ -165,9 +165,9 @@
             grad_shift_edge,
         ]
     )
-    summed = lax.psum(jnp.concatenate([edge_vec, node_vec]).astype(jnp.bfloat16), "cut").astype(
-        jnp.float32
-    )
+    summed = jnp.sum(
+        lax.all_gather(jnp.concatenate([edge_vec, node_vec]).astype(jnp.bfloat16), "cut"), axis=0
+    ).astype(jnp.float32)
     edge_summed = summed[: edge_vec.shape[0]]
     node_summed = summed[edge_vec.shape[0] :]
     param_grad = jnp.concatenate(

time: 508 us -> 447 us (0.88)
  waiting for transfers between devices: 222 us -> 146 us
  other arithmetic: 136 us -> 155 us
    psum x1 -> x0, waiting for transfers between devices: 136 us -> none  [per_device(): lax.psum(jnp.concatenate([edge_vec, node_vec]).astype(jnp.bfloat16), 'cut')]
    all_to_all x2, waiting for transfers between devices: 27.5 us -> 62 us  [reduce_mirrors(): lax.all_to_all(mirror_part.astype(jnp.bfloat16), 'cut', split_axis=1, con...]
    all_gather x0 -> x1, waiting for transfers between devices: none -> 24.8 us  [per_device(): lax.all_gather(jnp.concatenate([edge_vec, node_vec]).astype(jnp.bfloat16)...]
    reduce_sum x0 -> x1, other arithmetic: none -> 20.8 us  [per_device(): jnp.sum(lax.all_gather(jnp.concatenate([edge_vec, node_vec]).astype(jnp.b...]
    unnamed x99 -> x114, local copies, waits for them, and re-layouts: 14.8 us -> 11.1 us
  transfers between devices with their start and end apart: 6 -> 6, of which waited for: 5 -> 6; matrix products, arithmetic and copies ran while one was open for 2% -> 20% of each run, Pallas kernels for 0% -> 0%
where the time goes in v1:
time: 447 us; the launch traced here: 446 us
  other arithmetic  155 us (35%)
  waiting for transfers between devices  146 us (33%)
  local copies, waits for them, and re-layouts  83.6 us (19%)
  starting transfers between devices  30.9 us (7%)
  matrix products  15.4 us (3%)
  between operations  14.9 us (3%)
    all_to_all x2, waiting for transfers between devices, reduce_mirrors(): lax.all_to_all(mirror_part.astype(jnp.bfloat16), 'cut', split_axis=1, con...  62 us
    all_to_all x2, waiting for transfers between devices, fetch_mirrors(): lax.all_to_all(outgoing, 'cut', split_axis=1, concat_axis=1, tiled=True)  51 us
    scatter-add x2, other arithmetic, per_device(): grad_table = jnp.zeros((latent, local_width), jnp.float32).at[:, send_col...  47.1 us
    scatter-add x2, other arithmetic, reduce_mirrors(): result = master_part.at[:, mirror_index].add(returned)  46.1 us
    all_gather x1, waiting for transfers between devices, per_device(): lax.all_gather(jnp.concatenate([edge_vec, node_vec]).astype(jnp.bfloat16)...  24.8 us
    gather x2, local copies, waits for them, and re-layouts, fetch_mirrors(): outgoing = jnp.take(master_part, mirror_index, axis=1)  24.3 us
    scatter-add x1, other arithmetic, per_device(): jnp.zeros((latent, local_width), jnp.float32).at[:, recv_cols].add(message)  23.3 us
    reduce_sum x1, other arithmetic, per_device(): jnp.sum(lax.all_gather(jnp.concatenate([edge_vec, node_vec]).astype(jnp.b...  20.8 us
  transfers between devices with their start and end apart: 6, of which 6 were waited for; matrix products, arithmetic and copies ran while one was open for 20% of the time, Pallas kernels for 0%

profile of v1, /device:TPU:2, one launch (start us, length us, event | category | flops | bytes accessed | tf_op | source)
XLA Modules:
  0.0 445.6 jit_solution(6015282421839211149)
XLA Ops:
  7.2 11.5 %all-to-all-start = ((s32[32,1,128]{2,1,0:T(1,128)}), s32[32,1,128]{2,1,0:T(1,128)S(1)}, u32[]{:S(2)}, u32[]{:S(2)}) async-start(s32[32,1,128]{2,1,0:T(1,128)} %bitcast.172), calls=%async_computation | async-start | bytes 32768 | tf_op jit(solution)/shard_map/all_to_all | solution.py:64
  19.4 1.1 copy.38
  20.5 7.9 %all-to-all-done = s32[32,1,128]{2,1,0:T(1,128)S(1)} async-done(((s32[32,1,128]{2,1,0:T(1,128)}), s32[32,1,128]{2,1,0:T(1,128)S(1)}, u32[]{:S(2)}, u32[]{:S(2)}) %all-to-all-start) | async-done | bytes 16416 | tf_op jit(solution)/shard_map/all_to_all | solution.py:64
  28.4 12.1 %gather_fusion = bf16[4096,128]{1,0:T(8,128)(2,1)S(1)} fusion(bf16[128,1024]{0,1:T(8,128)(2,1)S(1)} %copy.38, s32[4096]{0:T(1024)S(1)} %fusion.49), kind=kCustom, calls=%fused_computation.clone | custom fusion | bytes 2113536 | tf_op jit(solution)/shard_map/jit(_take)/gather | solution.py:69
  40.6 2.9 broadcast_select_fusion.1
  43.5 4.1 all-to-all-start.1
  47.7 1.3 copy.36
  49.8 25.3 %all-to-all-done.1 = bf16[128,32,128]{0,2,1:T(8,128)(2,1)S(1)} async-done(((bf16[128,32,128]{0,2,1:T(8,128)(2,1)}), bf16[128,32,128]{0,2,1:T(8,128)(2,1)S(1)}, u32[]{:S(2)}, u32[]{:S(2)}) %all-to-all-start.1) | async-done | bytes 1048608 | tf_op jit(solution)/shard_map/all_to_all | solution.py:70
  75.2 12.1 %gather_fusion.1 = bf16[4096,128]{1,0:T(8,128)(2,1)S(1)} fusion(bf16[128,5120]{0,1:T(8,128)(2,1)S(1)} %pad_maximum_fusion.1, s32[4096]{0:T(1024)S(1)} %get-tuple-element.40), kind=kCustom, calls=%fused_computation.1.clone | custom fusion | bytes 2113536 | tf_op jit(solution)/shard_map/jit(_take)/gather | solution.py:93
  87.3 15.0 %gather_fusion.2 = bf16[4096,128]{1,0:T(8,128)(2,1)} fusion(bf16[128,5120]{0,1:T(8,128)(2,1)S(1)} %pad_maximum_fusion.1, s32[4096]{0:T(1024)S(1)} %get-tuple-element.41), kind=kCustom, calls=%fused_computation.3.clone | custom fusion | bytes 2113536 | tf_op jit(solution)/shard_map/jit(_take)/gather | solution.py:94
  102.4 2.1 select_bitcast_fusion.1
  104.6 2.1 select_bitcast_fusion
  106.8 2.3 multiply_convert_fusion
  110.0 0.8 copy-done.1
  111.3 1.9 copy.37
  113.2 23.3 %scatter_custom_fusion = f32[128,5120]{0,1:T(8,128)S(1)} fusion(s32[4096]{0:T(1024)S(1)} %bitcast.170, f32[4096,128]{1,0:T(8,128)} %copy.37, f32[]{:T(128)} %constant.27.clone.1), kind=kCustom, calls=%fused_computation.47 | custom fusion | flops 524288 | bytes 2621952 | tf_op jit(solution)/shard_map/scatter-add | solution.py:103
  136.5 1.1 slice.89
  137.5 5.1 %all-to-all-start.2 = ((bf16[128,32,128]{0,2,1:T(8,128)(2,1)}), bf16[128,32,128]{0,2,1:T(8,128)(2,1)}, u32[]{:S(2)}, u32[]{:S(2)}) async-start(bf16[128,32,128]{0,2,1:T(8,128)(2,1)} %bitcast.160), calls=%async_computation.2 | async-start | bytes 2097152 | tf_op jit(solution)/shard_map/all_to_all | solution.py:74
  142.8 27.5 %all-to-all-done.2 = bf16[128,32,128]{0,2,1:T(8,128)(2,1)} async-done(((bf16[128,32,128]{0,2,1:T(8,128)(2,1)}), bf16[128,32,128]{0,2,1:T(8,128)(2,1)}, u32[]{:S(2)}, u32[]{:S(2)}) %all-to-all-start.2) | async-done | bytes 1048608 | tf_op jit(solution)/shard_map/all_to_all | solution.py:74
  170.3 23.1 %scatter_custom_fusion.1 = f32[128,1024]{0,1:T(8,128)S(1)} fusion(f32[128,1024]{0,1:T(8,128)S(1)} %slice.66, s32[4096]{0:T(1024)S(1)} %bitcast.173, bf16[128,4096]{0,1:T(8,128)(2,1)} %bitcast.44), kind=kCustom, calls=%fused_computation.22 | custom fusion | flops 1048576 | bytes 1572864 | tf_op jit(solution)/shard_map/scatter-add | solution.py:77
  193.6 1.3 multiply_convert_fusion.1
  196.0 1.0 fusion.36
  197.0 0.9 fusion.63
  198.1 12.1 %gather_fusion.3 = bf16[4096,128]{1,0:T(8,128)(2,1)S(1)} fusion(bf16[128,1024]{0,1:T(8,128)(2,1)S(1)} %fusion.25, s32[4096]{0:T(1024)S(1)} %fusion.49), kind=kCustom, calls=%fused_computation.2.clone | custom fusion | bytes 2113536 | tf_op jit(solution)/shard_map/jit(_take)/gather | solution.py:69
  210.2 2.9 broadcast_select_fusion
  213.1 5.1 %all-to-all-start.3 = ((bf16[128,32,128]{0,2,1:T(8,128)(2,1)}), bf16[128,32,128]{0,2,1:T(8,128)(2,1)S(1)}, u32[]{:S(2)}, u32[]{:S(2)}) async-start(bf16[128,32,128]{0,2,1:T(8,128)(2,1)} %bitcast.158), calls=%async_computation.3 | async-start | bytes 2097152 | tf_op jit(solution)/shard_map/all_to_all | solution.py:70
  219.2 0.8 copy.49
  220.2 25.7 %all-to-all-done.3 = bf16[128,32,128]{0,2,1:T(8,128)(2,1)S(1)} async-done(((bf16[128,32,128]{0,2,1:T(8,128)(2,1)}), bf16[128,32,128]{0,2,1:T(8,128)(2,1)S(1)}, u32[]{:S(2)}, u32[]{:S(2)}) %all-to-all-start.3) | async-done | bytes 1048608 | tf_op jit(solution)/shard_map/all_to_all | solution.py:70
  246.0 15.0 %gather_fusion.4 = bf16[4096,128]{1,0:T(8,128)(2,1)} fusion(bf16[128,5120]{0,1:T(8,128)(2,1)S(1)} %pad_maximum_fusion.2, s32[4096]{0:T(1024)S(1)} %get-tuple-element.41), kind=kCustom, calls=%fused_computation.4.clone | custom fusion | bytes 2113536 | tf_op jit(solution)/shard_map/jit(_take)/gather | solution.py:137
  261.0 1.6 copy.40
  262.9 1.2 fusion.12
  265.8 1.2 copy-done.48
  267.0 1.0 fusion.59
  270.4 0.8 copy-done.20
  271.2 2.5 fusion.45
  273.7 23.3 %scatter_custom_fusion.2 = f32[128,5120]{0,1:T(8,128)S(1)} fusion(s32[4096]{0:T(1024)} %bitcast.175, f32[4096,128]{1,0:T(8,128)} %fusion.45, f32[]{:T(128)} %constant.27.clone.1), kind=kCustom, calls=%fused_computation.45 | custom fusion | flops 524288 | bytes 2621952 | tf_op jit(solution)/shard_map/scatter-add | solution.py:152
  297.0 3.0 fusion.43
  299.9 23.8 %scatter_fusion = f32[128,5120]{0,1:T(8,128)S(1)} fusion(f32[128,5120]{0,1:T(8,128)S(1)} %scatter_custom_fusion.2, s32[4096]{0:T(1024)S(1)} %bitcast.171, f32[4096,128]{1,0:T(8,128)} %fusion.43), kind=kCustom, calls=%fused_computation.8 | custom fusion | flops 524288 | bytes 6307840 | tf_op jit(solution)/shard_map/scatter-add | solution.py:154
  323.8 1.1 slice.88
  324.9 5.1 %all-to-all-start.4 = ((bf16[128,32,128]{0,2,1:T(8,128)(2,1)}), bf16[128,32,128]{0,2,1:T(8,128)(2,1)}, u32[]{:S(2)}, u32[]{:S(2)}) async-start(bf16[128,32,128]{0,2,1:T(8,128)(2,1)} %bitcast.159), calls=%async_computation.4 | async-start | bytes 2097152 | tf_op jit(solution)/shard_map/all_to_all | solution.py:74
  330.0 1.7 fusion.2
  331.7 1.3 copy.44
  333.7 34.5 %all-to-all-done.4 = bf16[128,32,128]{0,2,1:T(8,128)(2,1)} async-done(((bf16[128,32,128]{0,2,1:T(8,128)(2,1)}), bf16[128,32,128]{0,2,1:T(8,128)(2,1)}, u32[]{:S(2)}, u32[]{:S(2)}) %all-to-all-start.4) | async-done | bytes 1048608 | tf_op jit(solution)/shard_map/all_to_all | solution.py:74
  368.2 23.0 %scatter_custom_fusion.4 = f32[128,1024]{0,1:T(8,128)S(1)} fusion(f32[128,1024]{0,1:T(8,128)S(1)} %copy.42, s32[4096]{0:T(1024)} %bitcast.174, bf16[128,4096]{0,1:T(8,128)(2,1)} %bitcast.46), kind=kCustom, calls=%fused_computation.20 | custom fusion | flops 1048576 | bytes 1572864 | tf_op jit(solution)/shard_map/scatter-add | solution.py:77
  391.2 1.0 copy.43
  392.2 24.8 %all-gather.3.cloned.1.call-done = bf16[32,1,115456]{2,1,0:T(2,128)(2,1)} async-done(((bf16[1,1,115456]{2,1,0:T(2,128)(2,1)}), bf16[32,1,115456]{2,1,0:T(2,128)(2,1)}) %all-gather.3.cloned.1.call-update) | async-done | bytes 7389200 | tf_op jit(solution)/shard_map/all_gather | solution.py:169
  417.0 20.8 %reduce_sum.152 = bf16[115456]{0:T(1024)(128)(2,1)S(1)} reduce(bf16[32,1,115456]{2,1,0:T(2,128)(2,1)} %all-gather.3.cloned.1.call-done, bf16[]{:T(256)} %constant.57.clone.1), dimensions={0,1}, to_apply=%region_19.22 | reduce | flops 3579136 | bytes 7620098 | tf_op jit(solution)/shard_map/reduce_sum | solution.py:168
  438.0 0.8 pad_maximum_fusion.10
  (152 shorter events, 10.8 us)
Async XLA Ops:
  7.2 101.9 %copy-start = (bf16[128,128]{1,0:T(8,128)(2,1)S(1)}, bf16[128,128]{1,0:T(8,128)(2,1)}, u32[]{:S(2)}) copy-start(bf16[128,128]{1,0:T(8,128)(2,1)} %param.29) | copy-start | bytes 98308
  7.2 21.2 %all-to-all-start = ((s32[32,1,128]{2,1,0:T(1,128)}), s32[32,1,128]{2,1,0:T(1,128)S(1)}, u32[]{:S(2)}, u32[]{:S(2)}) async-start(s32[32,1,128]{2,1,0:T(1,128)} %bitcast.172), calls=%async_computation | async-start | bytes 32768 | tf_op jit(solution)/shard_map/all_to_all | solution.py:64
  40.6 7.0 %copy-start.40 = (s32[32,2]{0,1:T(2,128)S(1)}, s32[32,2]{0,1:T(2,128)}, u32[]{:S(2)}) copy-start(s32[32,2]{0,1:T(2,128)} %param.24) | copy-start | bytes 772
  43.5 4.2 copy-start.10
  43.5 5.5 %copy-start.34 = (s32[32,2,128]{2,1,0:T(2,128)S(1)}, s32[32,2,128]{2,1,0:T(2,128)}, u32[]{:S(2)}) copy-start(s32[32,2,128]{2,1,0:T(2,128)} %param.25) | copy-start | bytes 98308
  43.5 31.6 %all-to-all-start.1 = ((bf16[128,32,128]{0,2,1:T(8,128)(2,1)}), bf16[128,32,128]{0,2,1:T(8,128)(2,1)S(1)}, u32[]{:S(2)}, u32[]{:S(2)}) async-start(bf16[128,32,128]{0,2,1:T(8,128)(2,1)} %bitcast.156), calls=%async_computation.1 | async-start | bytes 2097152 | tf_op jit(solution)/shard_map/all_to_all | solution.py:70
  49.1 55.4 %copy-start.30 = (pred[4096]{0:T(1024)(128)(4,1)}, pred[4096]{0:T(1024)(128)(4,1)S(1)}, u32[]{:S(2)}) copy-start(pred[4096]{0:T(1024)(128)(4,1)S(1)} %compare_and_fusion) | copy-start | bytes 12292
  49.8 63.4 %copy-start.26 = (s32[4096,1]{0,1:T(1,128)}, s32[4096,1]{0,1:T(1,128)S(1)}, u32[]{:S(2)}) copy-start(s32[4096,1]{0,1:T(1,128)S(1)} %get-tuple-element.26) | copy-start | bytes 49156
  102.4 2.2 copy-start.6
  102.4 4.4 copy-start.11
  102.4 4.4 copy-start.24
  102.4 4.4 copy-start.45
  104.6 4.5 %copy-start.13 = (bf16[128,4096]{0,1:T(8,128)(2,1)}, bf16[128,4096]{0,1:T(8,128)(2,1)S(1)}, u32[]{:S(2)}) copy-start(bf16[128,4096]{0,1:T(8,128)(2,1)S(1)} %select_bitcast_fusion.1) | copy-start | bytes 3145732
  106.8 2.3 copy-start.15
  109.1 1.8 copy-start.36
  109.1 1.8 copy-start.41
  109.5 1.3 copy-start.1
  137.5 32.7 %all-to-all-start.2 = ((bf16[128,32,128]{0,2,1:T(8,128)(2,1)}), bf16[128,32,128]{0,2,1:T(8,128)(2,1)}, u32[]{:S(2)}, u32[]{:S(2)}) async-start(bf16[128,32,128]{0,2,1:T(8,128)(2,1)} %bitcast.160), calls=%async_computation.2 | async-start | bytes 2097152 | tf_op jit(solution)/shard_map/all_to_all | solution.py:74
  142.7 50.8 %copy-start.46 = (f32[128]{0:T(128)S(1)}, f32[128]{0:T(128)}, u32[]{:S(2)}) copy-start(f32[128]{0:T(128)} %param.33) | copy-start | bytes 1540
  142.7 52.1 %copy-start.35 = (s32[4096,1]{0,1:T(1,128)}, s32[4096,1]{0,1:T(1,128)S(1)}, u32[]{:S(2)}) copy-start(s32[4096,1]{0,1:T(1,128)S(1)} %compare_select_fusion.1) | copy-start | bytes 49156
  193.4 1.4 copy-start.33
  193.5 1.6 copy-start.22
  193.5 1.7 copy-start.7
  193.5 1.7 copy-start.39
  193.5 2.4 copy-start.17
  193.5 2.4 copy-start.42
  196.0 1.9 copy-start.28
  197.9 21.0 %copy-start.8 = (bf16[128,1024]{0,1:T(8,128)(2,1)}, bf16[128,1024]{0,1:T(8,128)(2,1)S(1)}, u32[]{:S(2)}) copy-start(bf16[128,1024]{0,1:T(8,128)(2,1)S(1)} %get-tuple-element.39) | copy-start | bytes 786436
  213.1 5.8 %copy-start.23 = (bf16[128,1024]{0,1:T(8,128)(2,1)S(1)}, bf16[128,1024]{0,1:T(8,128)(2,1)}, u32[]{:S(2)}) copy-start(bf16[128,1024]{0,1:T(8,128)(2,1)} %copy-done.22) | copy-start | bytes 786436
  213.1 6.8 %copy-start.19 = (bf16[128,1024]{1,0:T(8,128)(2,1)S(1)}, bf16[128,1024]{1,0:T(8,128)(2,1)}, u32[]{:S(2)}) copy-start(bf16[128,1024]{1,0:T(8,128)(2,1)} %copy-done.18) | copy-start | bytes 786436
  213.1 32.8 %all-to-all-start.3 = ((bf16[128,32,128]{0,2,1:T(8,128)(2,1)}), bf16[128,32,128]{0,2,1:T(8,128)(2,1)S(1)}, u32[]{:S(2)}, u32[]{:S(2)}) async-start(bf16[128,32,128]{0,2,1:T(8,128)(2,1)} %bitcast.158), calls=%async_computation.3 | async-start | bytes 2097152 | tf_op jit(solution)/shard_map/all_to_all | solution.py:70
  218.2 198.8 %all-gather.3.cloned.1.call-start = ((), (), s32[]{:S(2)}) async-start(), calls=%async_computation.5 | async-start | bytes 15240192 | tf_op jit(solution)/shard_map/all_gather | solution.py:169
  246.0 16.7 %copy-start.31 = (pred[4096]{0:T(1024)(128)(4,1)S(1)}, pred[4096]{0:T(1024)(128)(4,1)}, u32[]{:S(2)}) copy-start(pred[4096]{0:T(1024)(128)(4,1)} %copy-done.30) | copy-start | bytes 12292
  246.0 16.7 %copy-start.37 = (f32[128]{0:T(128)S(1)}, f32[128]{0:T(128)}, u32[]{:S(2)}) copy-start(f32[128]{0:T(128)} %param.30) | copy-start | bytes 1540
  261.0 1.9 copy-start.2
  265.4 1.6 copy-start.48
  267.0 1.5 copy-start.14
  267.0 1.9 copy-start.16
  268.0 3.2 copy-start.3
  268.8 1.3 copy-start.21
  268.8 1.4 copy-start.47
  268.8 1.5 copy-start.43
  268.8 1.5 copy-start.44
  273.7 23.3 %copy-start.25 = (bf16[128,384]{1,0:T(8,128)(2,1)S(1)}, bf16[128,384]{1,0:T(8,128)(2,1)}, u32[]{:S(2)}) copy-start(bf16[128,384]{1,0:T(8,128)(2,1)} %param.27) | copy-start | bytes 294916
  297.0 3.0 copy-start.27
  324.9 43.4 %all-to-all-start.4 = ((bf16[128,32,128]{0,2,1:T(8,128)(2,1)}), bf16[128,32,128]{0,2,1:T(8,128)(2,1)}, u32[]{:S(2)}, u32[]{:S(2)}) async-start(bf16[128,32,128]{0,2,1:T(8,128)(2,1)} %bitcast.159), calls=%async_computation.4 | async-start | bytes 2097152 | tf_op jit(solution)/shard_map/all_to_all | solution.py:74
  331.7 1.5 copy-start.9
  331.7 1.5 copy-start.29
  (7 other events, 7.5 us)
Sparse Core Ops, SparseCore 0:
  271.3 145.6 all-gather.2
